TPU v7x, 32 devices: a whole 2x2x4 slice. The times are simulated.
32 devices in a mesh: row: 4 (over y, x), col: 8 (over z, core).
Axes of the slice: x: 2, y: 2, z: 4, core: 2. Of those that a mesh axis runs over, the one named last changes fastest.
Arguments:
- rhs: float32 [4, 8, 4608], P('row', 'col'), may hold values from -14 to 14
- friction: float32 [4, 8, 4608], P('row', 'col'), may hold values from 1 to 4
- kernel_tiles: bfloat16 [4, 8, 256, 128, 128], P('row', 'col'), may hold values from -0.1875 to 0.1875
- tile_scale: float32 [4, 8, 256], P('row', 'col'), may hold values from 0.5 to 2
- tile_row: int32 [4, 8, 256], P('row', 'col'), may hold values from 0 to 287, as said below
- tile_col: int32 [4, 8, 256], P('row', 'col'), may hold values from 0 to 143
- tile_counts: int32 [4, 8], P('row', 'col'), may hold values from 64 to 256, as said below
- precond_blocks: bfloat16 [4, 8, 24, 512, 512], P('row', 'col'), may hold values from -3 to 3, as said below
- fault_sizes: int32 [4, 8, 24], P('row', 'col'), may hold values from 1 to 512, 4608 in all within a row
Outputs:
- update: float32 [4, 8, 4608], P('row', 'col')
- residual: float32 [4, 8, 4608], P('row', 'col')
Inputs may be any that keep to these rules, and one draw needn't show every extreme that they name: Row tile within the row group; in every block (r, c), over all 256 slots, at most 64 slots have the same tile_row // 36, and some value of it has exactly 64. `tile_counts`: slots at or beyond the count hold no kernel tile and are ignored; some block has 256 live slots and some 256 // 4. `fault_sizes`: the faults of each (r, c) cover its 4608 elements in order; each (r, c) has a fault of exactly 512 elements. `precond_blocks`: entries of a block outside its fault's size are ignored.
All inputs are finite; a program needn't handle non-finite values.
Results may differ from a plain program's by a relative error of at most 0.012.
Values may be sent and summed in bfloat16 or wider, within the bound.
No kernel may reach another device: no remote copies, remote signals or barrier semaphores. Data moves between devices by JAX's collectives and lax.ppermute only.
A program may use at most 64 MiB of HBM per device.

v0:
```python
import jax
import jax.numpy as jnp
from jax import lax
from jax.sharding import PartitionSpec as P

ITERS = 3
exact_mode = lax.Precision.HIGHEST


def local(
    rhs,
    friction,
    kernel_tiles,
    tile_scale,
    tile_row,
    tile_col,
    tile_counts,
    precond_blocks,
    fault_sizes,
):
    vector_len = rhs.shape[2]
    tile_width = kernel_tiles.shape[3]
    slot_count = kernel_tiles.shape[2]
    fault_width = precond_blocks.shape[3]
    col_devices = lax.axis_size("col")
    row_tiles = col_devices * vector_len // tile_width
    local_tiles = kernel_tiles[0, 0]
    tile_rows = tile_row[0, 0]
    tile_cols = tile_col[0, 0]
    tile_weight = jnp.where(
        jnp.arange(slot_count, dtype=jnp.int32) < tile_counts[0, 0], tile_scale[0, 0], 0.0
    )
    fault_blocks = precond_blocks[0, 0]
    fault_len = fault_sizes[0, 0]
    fault_starts = jnp.cumsum(fault_len) - fault_len
    slot_place = jnp.arange(fault_width, dtype=jnp.int32)
    gather_spot = jnp.clip(fault_starts[:, None] + slot_place[None, :], 0, vector_len - 1)
    slot_live = slot_place[None, :] < fault_len[:, None]
    element_ids = jnp.arange(vector_len, dtype=jnp.int32)
    owner_fault = (
        jnp.sum((fault_starts[None, :] <= element_ids[:, None]).astype(jnp.int32), axis=1) - 1
    )
    flat_spot = owner_fault * fault_width + element_ids - fault_starts[owner_fault]

    def kernel_apply(field):
        low_field = field.astype(jnp.bfloat16).reshape(1, 1, vector_len)
        column = lax.all_gather(low_field, "row", axis=0, tiled=True)
        column_pieces = column.reshape(-1, tile_width)[tile_cols]
        products = (
            jnp.einsum("tij,tj->ti", local_tiles, column_pieces, preferred_element_type=jnp.float32)
            * tile_weight[:, None]
        )
        partial_value = jax.ops.segment_sum(products, tile_rows, num_segments=row_tiles).reshape(-1)
        row_total = lax.psum(partial_value, "col")
        return lax.dynamic_slice_in_dim(row_total, lax.axis_index("col") * vector_len, vector_len)

    rhs_flat = rhs.reshape(-1)
    friction_flat = friction.reshape(-1)

    def operator(field):
        return friction_flat * field + kernel_apply(field)

    def global_norm(field):
        return jnp.sqrt(lax.psum(jnp.sum(field * field), ("row", "col")))

    rhs_norm = global_norm(rhs_flat)
    krylov = [rhs_flat / rhs_norm]
    directions = []
    hessenberg = jnp.zeros((ITERS + 1, ITERS), jnp.float32)
    for step in range(ITERS):
        low_vector = krylov[step].astype(jnp.bfloat16)
        padded = jnp.where(slot_live, low_vector[gather_spot], jnp.zeros((), jnp.bfloat16))
        result = jnp.einsum("fij,fj->fi", fault_blocks, padded, preferred_element_type=jnp.float32)
        direction = result.reshape(-1)[flat_spot]
        directions.append(direction)
        image = operator(direction)
        height_list = []
        for earlier in krylov:
            height = lax.psum(jnp.sum(earlier * image), ("row", "col"))
            image = image - height * earlier
            height_list.append(height)
        heights = jnp.stack(height_list)
        new_norm = global_norm(image)
        hessenberg = hessenberg.at[: step + 1, step].set(heights).at[step + 1, step].set(new_norm)
        krylov.append(image / new_norm)
    gram_matrix = jnp.dot(hessenberg.T, hessenberg, precision=exact_mode)
    target = rhs_norm * hessenberg[0, :]
    lower_factor = jnp.linalg.cholesky(gram_matrix)
    weights_y = jax.scipy.linalg.cho_solve((lower_factor, True), target)
    update = jnp.dot(weights_y, jnp.stack(directions), precision=exact_mode)
    residual = rhs_flat - operator(update)
    return (update.reshape(1, 1, vector_len), residual.reshape(1, 1, vector_len))


def solution(mesh):
    return jax.shard_map(
        local,
        mesh=mesh,
        in_specs=(
            P("row", "col", None),
            P("row", "col", None),
            P("row", "col", None, None, None),
            P("row", "col", None),
            P("row", "col", None),
            P("row", "col", None),
            P("row", "col"),
            P("row", "col", None, None, None),
            P("row", "col", None),
        ),
        out_specs=(P("row", "col", None), P("row", "col", None)),
        check_vma=False,
    )
```

profile of v0, /device:TPU:8, one launch (start us, length us, event | category | flops | bytes accessed | tf_op | source)
XLA Modules:
  0.0 1087.3 jit_solution(13645294912561519744)
XLA Ops:
  15.8 10.6 select_select_fusion
  27.9 40.7 %psum.98 = f32[]{:T(128)} all-reduce(f32[]{:T(128)} %multiply_reduce_fusion.9), channel_id=1, replica_groups=mesh['row'=4,'col'=8] {'row','col'}, use_global_device_ids=true, to_apply=%region_1.2 | all-reduce | flops 1 | bytes 8 | tf_op jit(solution)/shard_map/psum | solution.py:64
  69.4 75.8 %gather_fusion = bf16[12288]{0:T(1024)(128)(2,1)S(1)} fusion(bf16[4608]{0:T(1024)(128)(2,1)S(1)} %fusion.59, s32[12288]{0:T(1024)S(1)} %broadcast_clamp_fusion), kind=kCustom, calls=%fused_computation | custom fusion | bytes 98304 | tf_op jit(solution)/shard_map/gather | solution.py:72
  145.3 7.9 fusion.4
  153.3 24.1 %gather_fusion.1 = f32[4608]{0:T(1024)S(1)} fusion(f32[12288]{0:T(1024)S(1)} %bitcast.140, s32[5120]{0:T(1024)S(1)} %pad_clamp_fusion), kind=kCustom, calls=%fused_computation.1 | custom fusion | bytes 55296 | tf_op jit(solution)/shard_map/gather | solution.py:74
  177.4 9.3 all-gather.4
  188.5 7.8 fusion.12
  200.6 50.8 %all-reduce.6.cloned.1.call-done = f32[36864]{0:T(1024)} async-done(((f32[36864]{0:T(1024)}), f32[36864]{0:T(1024)}) %all-reduce.6.cloned.1.call-update) | async-done | bytes 147472 | tf_op jit(solution)/shard_map/psum | solution.py:54
  252.8 39.5 %psum.100 = f32[]{:T(128)} all-reduce(f32[]{:T(128)} %get-tuple-element.99), channel_id=1, replica_groups=mesh['row'=4,'col'=8] {'row','col'}, use_global_device_ids=true, to_apply=%region_7.8 | all-reduce | flops 1 | bytes 8 | tf_op jit(solution)/shard_map/psum | solution.py:79
  293.5 40.7 %psum.101 = f32[]{:T(128)} all-reduce(f32[]{:T(128)} %multiply_reduce_fusion.7), channel_id=1, replica_groups=mesh['row'=4,'col'=8] {'row','col'}, use_global_device_ids=true, to_apply=%region_9.10 | all-reduce | flops 1 | bytes 8 | tf_op jit(solution)/shard_map/psum | solution.py:64
  335.6 75.8 %gather_fusion.3 = bf16[12288]{0:T(1024)(128)(2,1)S(1)} fusion(bf16[4608]{0:T(1024)(128)(2,1)S(1)} %fusion.60, s32[12288]{0:T(1024)S(1)} %broadcast_clamp_fusion), kind=kCustom, calls=%fused_computation.3 | custom fusion | bytes 98304 | tf_op jit(solution)/shard_map/gather | solution.py:72
  411.5 7.9 fusion.2
  419.5 24.1 %gather_fusion.4 = f32[4608]{0:T(1024)S(1)} fusion(f32[12288]{0:T(1024)S(1)} %bitcast.141, s32[5120]{0:T(1024)S(1)} %pad_clamp_fusion), kind=kCustom, calls=%fused_computation.4 | custom fusion | bytes 55296 | tf_op jit(solution)/shard_map/gather | solution.py:74
  443.6 9.3 all-gather.5
  454.0 7.8 fusion.10
  465.5 51.4 %all-reduce.8.cloned.1.call-done = f32[36864]{0:T(1024)} async-done(((f32[36864]{0:T(1024)}), f32[36864]{0:T(1024)}) %all-reduce.8.cloned.1.call-update) | async-done | bytes 147472 | tf_op jit(solution)/shard_map/psum | solution.py:54
  518.4 39.5 %psum.103 = f32[]{:T(128)} all-reduce(f32[]{:T(128)} %get-tuple-element.97), channel_id=1, replica_groups=mesh['row'=4,'col'=8] {'row','col'}, use_global_device_ids=true, to_apply=%region_14.15 | all-reduce | flops 1 | bytes 8 | tf_op jit(solution)/shard_map/psum | solution.py:79
  559.9 40.6 %psum.104 = f32[]{:T(128)} all-reduce(f32[]{:T(128)} %multiply_reduce_fusion.5), channel_id=1, replica_groups=mesh['row'=4,'col'=8] {'row','col'}, use_global_device_ids=true, to_apply=%region_16.17 | all-reduce | flops 1 | bytes 8 | tf_op jit(solution)/shard_map/psum | solution.py:79
  603.2 40.5 %psum.105 = f32[]{:T(128)} all-reduce(f32[]{:T(128)} %get-tuple-element.95), channel_id=1, replica_groups=mesh['row'=4,'col'=8] {'row','col'}, use_global_device_ids=true, to_apply=%region_18.19 | all-reduce | flops 1 | bytes 8 | tf_op jit(solution)/shard_map/psum | solution.py:64
  644.4 75.8 %gather_fusion.6 = bf16[12288]{0:T(1024)(128)(2,1)S(1)} fusion(bf16[4608]{0:T(1024)(128)(2,1)S(1)} %fusion.58, s32[12288]{0:T(1024)S(1)} %broadcast_clamp_fusion), kind=kCustom, calls=%fused_computation.6 | custom fusion | bytes 98304 | tf_op jit(solution)/shard_map/gather | solution.py:72
  720.3 7.9 fusion
  728.3 24.1 %gather_fusion.7 = f32[4608]{0:T(1024)S(1)} fusion(f32[12288]{0:T(1024)S(1)} %bitcast.139, s32[5120]{0:T(1024)S(1)} %pad_clamp_fusion), kind=kCustom, calls=%fused_computation.7 | custom fusion | bytes 55296 | tf_op jit(solution)/shard_map/gather | solution.py:74
  752.4 9.5 all-gather.6
  763.0 7.8 fusion.8
  776.4 50.5 %all-reduce.10.cloned.1.call-done = f32[36864]{0:T(1024)} async-done(((f32[36864]{0:T(1024)}), f32[36864]{0:T(1024)}) %all-reduce.10.cloned.1.call-update) | async-done | bytes 147472 | tf_op jit(solution)/shard_map/psum | solution.py:54
  828.4 39.5 %psum.107 = f32[]{:T(128)} all-reduce(f32[]{:T(128)} %get-tuple-element.93), channel_id=1, replica_groups=mesh['row'=4,'col'=8] {'row','col'}, use_global_device_ids=true, to_apply=%region_23.24 | all-reduce | flops 1 | bytes 8 | tf_op jit(solution)/shard_map/psum | solution.py:79
  871.1 40.6 %psum.108 = f32[]{:T(128)} all-reduce(f32[]{:T(128)} %multiply_reduce_fusion.2), channel_id=1, replica_groups=mesh['row'=4,'col'=8] {'row','col'}, use_global_device_ids=true, to_apply=%region_25.26 | all-reduce | flops 1 | bytes 8 | tf_op jit(solution)/shard_map/psum | solution.py:79
  914.2 40.4 %psum.109 = f32[]{:T(128)} all-reduce(f32[]{:T(128)} %get-tuple-element.91), channel_id=1, replica_groups=mesh['row'=4,'col'=8] {'row','col'}, use_global_device_ids=true, to_apply=%region_27.28 | all-reduce | flops 1 | bytes 8 | tf_op jit(solution)/shard_map/psum | solution.py:79
  955.9 40.5 %psum.110 = f32[]{:T(128)} all-reduce(f32[]{:T(128)} %multiply_reduce_fusion), channel_id=1, replica_groups=mesh['row'=4,'col'=8] {'row','col'}, use_global_device_ids=true, to_apply=%region_29.30 | all-reduce | flops 1 | bytes 8 | tf_op jit(solution)/shard_map/psum | solution.py:64
  1006.1 9.3 all-gather.7
  1016.4 7.8 fusion.6
  1026.5 52.8 %all-reduce.12.cloned.1.call-done = f32[36864]{0:T(1024)} async-done(((f32[36864]{0:T(1024)}), f32[36864]{0:T(1024)}) %all-reduce.12.cloned.1.call-update) | async-done | bytes 147472 | tf_op jit(solution)/shard_map/psum | solution.py:54
  (118 shorter events, 59.4 us)
Async XLA Ops:
  7.2 244.2 %all-reduce.6.cloned.1.call-start = ((), (), s32[]{:S(2)}) async-start(), calls=%async_computation | async-start | bytes 294912 | tf_op jit(solution)/shard_map/psum | solution.py:54
  69.4 75.9 %copy-start.1 = (s32[1,1,24]{2,1,0:T(1,128)S(1)}, s32[1,1,24]{2,1,0:T(1,128)}, u32[]{:S(2)}) copy-start(s32[1,1,24]{2,1,0:T(1,128)} %param.29) | copy-start | bytes 292
  153.3 33.7 %copy-start.2 = (s32[1,1,256]{2,1,0:T(1,128)S(1)}, s32[1,1,256]{2,1,0:T(1,128)}, u32[]{:S(2)}) copy-start(s32[1,1,256]{2,1,0:T(1,128)} %param.26) | copy-start | bytes 3076
  177.4 18.9 %copy-start.3 = (f32[1,1,256]{2,1,0:T(1,128)S(1)}, f32[1,1,256]{2,1,0:T(1,128)}, u32[]{:S(2)}) copy-start(f32[1,1,256]{2,1,0:T(1,128)} %param.24) | copy-start | bytes 3076
  177.4 21.9 %copy-start = (f32[1,1,4608]{2,1,0:T(1,128)S(1)}, f32[1,1,4608]{2,1,0:T(1,128)}, u32[]{:S(2)}) copy-start(f32[1,1,4608]{2,1,0:T(1,128)} %param.22) | copy-start | bytes 55300
  177.4 22.6 %copy-start.4 = (s32[2]{0:T(128)S(1)}, s32[2]{0:T(128)}, u32[]{:S(2)}) copy-start(s32[2]{0:T(128)} %constant.236.clone.1) | copy-start | bytes 28
  198.6 318.3 %all-reduce.8.cloned.1.call-start = ((), (), s32[]{:S(2)}) async-start(), calls=%async_computation.1 | async-start | bytes 294912 | tf_op jit(solution)/shard_map/psum | solution.py:54
  464.1 362.8 %all-reduce.10.cloned.1.call-start = ((), (), s32[]{:S(2)}) async-start(), calls=%async_computation.2 | async-start | bytes 294912 | tf_op jit(solution)/shard_map/psum | solution.py:54
  773.1 306.2 %all-reduce.12.cloned.1.call-start = ((), (), s32[]{:S(2)}) async-start(), calls=%async_computation.3 | async-start | bytes 294912 | tf_op jit(solution)/shard_map/psum | solution.py:54
Sparse Core Ops, SparseCore 0:
  198.7 52.6 all-reduce.5
  464.2 52.6 all-reduce.7
  773.2 53.5 all-reduce.9
  1026.6 52.6 all-reduce.11
where the time goes:
time: 1090 us
  blocking collectives  440 us (40%)
  local copies, waits for them, and re-layouts  311 us (29%)
  waiting for transfers between devices  206 us (19%)
  other arithmetic  56.7 us (5%)
  matrix products  56.1 us (5%)
  between operations  17.6 us (2%)
    psum x6, blocking collectives, local(): height = lax.psum(jnp.sum(earlier * image), ('row', 'col'))  240 us
    gather x6, local copies, waits for them, and re-layouts, local(): low_vector[gather_spot]  228 us
    psum x4, waiting for transfers between devices, kernel_apply(): row_total = lax.psum(partial_value, 'col')  206 us
    psum x4, blocking collectives, global_norm(): return jnp.sqrt(lax.psum(jnp.sum(field * field), ('row', 'col')))  162 us
    gather x3, local copies, waits for them, and re-layouts, local(): direction = result.reshape(-1)[flat_spot]  72.2 us
    all_gather x4, blocking collectives, kernel_apply(): column = lax.all_gather(low_field, 'row', axis=0, tiled=True)  37.3 us
    dot_general x4, matrix products, kernel_apply(): jnp.einsum('tij,tj->ti', local_tiles, column_pieces, preferred_element_ty...  31.1 us
    dot_general x3, matrix products, local(): jnp.einsum('fij,fj->fi', fault_blocks, padded, preferred_element_type=jnp...  23.7 us
  transfers between devices with their start and end apart: 4, of which 4 were waited for; matrix products, arithmetic and copies ran while one was open for 1% of the time, Pallas kernels for 0%

commit v1 on v0

--- a/solution.py
+++ b/solution.py
@@ -51,7 +51,7 @@
             * tile_weight[:, None]
         )
         partial_value = jax.ops.segment_sum(products, tile_rows, num_segments=row_tiles).reshape(-1)
-        row_total = lax.psum(partial_value, "col")
+        row_total = lax.all_gather(partial_value, "col").sum(axis=0)
         return lax.dynamic_slice_in_dim(row_total, lax.axis_index("col") * vector_len, vector_len)
 
     rhs_flat = rhs.reshape(-1)

time: 1090 us -> 972 us (0.89)
  waiting for transfers between devices: 206 us -> 80.6 us
    psum x4 -> x0, waiting for transfers between devices: 206 us -> none  [kernel_apply(): row_total = lax.psum(partial_value, 'col')]
    all_gather x0 -> x4, waiting for transfers between devices: none -> 80.6 us  [kernel_apply(): row_total = lax.all_gather(partial_value, 'col').sum(axis=0)]
where the time goes in v1:
time: 972 us; the launch traced here: 968 us
  blocking collectives  439 us (45%)
  local copies, waits for them, and re-layouts  311 us (32%)
  waiting for transfers between devices  80.6 us (8%)
  other arithmetic  62.3 us (6%)
  matrix products  56.1 us (6%)
  between operations  17.7 us (2%)
    psum x6, blocking collectives, local(): height = lax.psum(jnp.sum(earlier * image), ('row', 'col'))  240 us
    gather x6, local copies, waits for them, and re-layouts, local(): low_vector[gather_spot]  228 us
    psum x4, blocking collectives, global_norm(): return jnp.sqrt(lax.psum(jnp.sum(field * field), ('row', 'col')))  162 us
    all_gather x4, waiting for transfers between devices, kernel_apply(): row_total = lax.all_gather(partial_value, 'col').sum(axis=0)  80.6 us
    gather x3, local copies, waits for them, and re-layouts, local(): direction = result.reshape(-1)[flat_spot]  72.2 us
    all_gather x4, blocking collectives, kernel_apply(): column = lax.all_gather(low_field, 'row', axis=0, tiled=True)  37.5 us
    dot_general x4, matrix products, kernel_apply(): jnp.einsum('tij,tj->ti', local_tiles, column_pieces, preferred_element_ty...  31.1 us
    dot_general x3, matrix products, local(): jnp.einsum('fij,fj->fi', fault_blocks, padded, preferred_element_type=jnp...  23.7 us
  transfers between devices with their start and end apart: 4, of which 4 were waited for; matrix products, arithmetic and copies ran while one was open for 1% of the time, Pallas kernels for 0%

profile of v1, /device:TPU:8, one launch (start us, length us, event | category | flops | bytes accessed | tf_op | source)
XLA Modules:
  0.0 967.5 jit_solution(16016314623661135520)
XLA Ops:
  15.8 10.6 %select_select_fusion = s32[4608]{0:T(1024)S(1)} fusion(pred[4608]{0:T(1024)(128)(4,1)S(1)} %get-tuple-element.90, pred[4608]{0:T(1024)(128)(4,1)S(1)} %get-tuple-element.89, pred[4608]{0:T(1024)(128)(4,1)S(1)} %get-tuple-element.88, pred[4608]{0:T(1024)(128)(4,1)S(1)} %get-tuple-element.87, pred[4608]{0:T(1024)(128)(4,1)S(1)} %get-tuple-element.86, ...), kind=kLoop, calls=%fused_computation.100 | loop fusion | flops 78336 | bytes 115268 | tf_op jit(solution)/shard_map/gather | solution.py:43
  27.9 40.7 %psum.70 = f32[]{:T(128)} all-reduce(f32[]{:T(128)} %multiply_reduce_fusion.9), channel_id=1, replica_groups=mesh['row'=4,'col'=8] {'row','col'}, use_global_device_ids=true, to_apply=%region_1.2 | all-reduce | flops 1 | bytes 8 | tf_op jit(solution)/shard_map/psum | solution.py:64
  69.4 75.8 %gather_fusion = bf16[12288]{0:T(1024)(128)(2,1)S(1)} fusion(bf16[4608]{0:T(1024)(128)(2,1)S(1)} %fusion.59, s32[12288]{0:T(1024)S(1)} %broadcast_clamp_fusion), kind=kCustom, calls=%fused_computation | custom fusion | bytes 98304 | tf_op jit(solution)/shard_map/gather | solution.py:72
  145.3 7.9 fusion.4
  153.3 24.1 %gather_fusion.1 = f32[4608]{0:T(1024)S(1)} fusion(f32[12288]{0:T(1024)S(1)} %bitcast.140, s32[5120]{0:T(1024)S(1)} %pad_clamp_fusion), kind=kCustom, calls=%fused_computation.1 | custom fusion | bytes 55296 | tf_op jit(solution)/shard_map/gather | solution.py:74
  177.4 9.3 all-gather.4
  188.5 7.8 fusion.12
  198.7 21.6 %all-gather.17.cloned.1.call-done = f32[8,1,36864]{2,1,0:T(1,128)} async-done(((f32[1,1,36864]{2,1,0:T(1,128)}), f32[8,1,36864]{2,1,0:T(1,128)}) %all-gather.17.cloned.1.call-update) | async-done | bytes 1179664 | tf_op jit(solution)/shard_map/all_gather | solution.py:54
  223.2 39.4 %psum.71 = f32[]{:T(128)} all-reduce(f32[]{:T(128)} %get-tuple-element.99), channel_id=1, replica_groups=mesh['row'=4,'col'=8] {'row','col'}, use_global_device_ids=true, to_apply=%region_7.8 | all-reduce | flops 1 | bytes 8 | tf_op jit(solution)/shard_map/psum | solution.py:79
  263.8 40.5 %psum.72 = f32[]{:T(128)} all-reduce(f32[]{:T(128)} %multiply_reduce_fusion.7), channel_id=1, replica_groups=mesh['row'=4,'col'=8] {'row','col'}, use_global_device_ids=true, to_apply=%region_9.10 | all-reduce | flops 1 | bytes 8 | tf_op jit(solution)/shard_map/psum | solution.py:64
  305.7 75.8 %gather_fusion.3 = bf16[12288]{0:T(1024)(128)(2,1)S(1)} fusion(bf16[4608]{0:T(1024)(128)(2,1)S(1)} %fusion.60, s32[12288]{0:T(1024)S(1)} %broadcast_clamp_fusion), kind=kCustom, calls=%fused_computation.3 | custom fusion | bytes 98304 | tf_op jit(solution)/shard_map/gather | solution.py:72
  381.6 7.9 fusion.2
  389.6 24.1 %gather_fusion.4 = f32[4608]{0:T(1024)S(1)} fusion(f32[12288]{0:T(1024)S(1)} %bitcast.141, s32[5120]{0:T(1024)S(1)} %pad_clamp_fusion), kind=kCustom, calls=%fused_computation.4 | custom fusion | bytes 55296 | tf_op jit(solution)/shard_map/gather | solution.py:74
  413.7 9.3 all-gather.6
  424.1 7.8 fusion.10
  434.2 21.6 %all-gather.19.cloned.1.call-done = f32[8,1,36864]{2,1,0:T(1,128)} async-done(((f32[1,1,36864]{2,1,0:T(1,128)}), f32[8,1,36864]{2,1,0:T(1,128)}) %all-gather.19.cloned.1.call-update) | async-done | bytes 1179664 | tf_op jit(solution)/shard_map/all_gather | solution.py:54
  458.7 39.4 %psum.73 = f32[]{:T(128)} all-reduce(f32[]{:T(128)} %get-tuple-element.97), channel_id=1, replica_groups=mesh['row'=4,'col'=8] {'row','col'}, use_global_device_ids=true, to_apply=%region_14.15 | all-reduce | flops 1 | bytes 8 | tf_op jit(solution)/shard_map/psum | solution.py:79
  500.1 40.4 %psum.74 = f32[]{:T(128)} all-reduce(f32[]{:T(128)} %multiply_reduce_fusion.5), channel_id=1, replica_groups=mesh['row'=4,'col'=8] {'row','col'}, use_global_device_ids=true, to_apply=%region_16.17 | all-reduce | flops 1 | bytes 8 | tf_op jit(solution)/shard_map/psum | solution.py:79
  543.0 40.5 %psum.75 = f32[]{:T(128)} all-reduce(f32[]{:T(128)} %get-tuple-element.95), channel_id=1, replica_groups=mesh['row'=4,'col'=8] {'row','col'}, use_global_device_ids=true, to_apply=%region_18.19 | all-reduce | flops 1 | bytes 8 | tf_op jit(solution)/shard_map/psum | solution.py:64
  584.2 75.8 %gather_fusion.6 = bf16[12288]{0:T(1024)(128)(2,1)S(1)} fusion(bf16[4608]{0:T(1024)(128)(2,1)S(1)} %fusion.58, s32[12288]{0:T(1024)S(1)} %broadcast_clamp_fusion), kind=kCustom, calls=%fused_computation.6 | custom fusion | bytes 98304 | tf_op jit(solution)/shard_map/gather | solution.py:72
  660.2 7.9 fusion
  668.1 24.1 %gather_fusion.7 = f32[4608]{0:T(1024)S(1)} fusion(f32[12288]{0:T(1024)S(1)} %bitcast.139, s32[5120]{0:T(1024)S(1)} %pad_clamp_fusion), kind=kCustom, calls=%fused_computation.7 | custom fusion | bytes 55296 | tf_op jit(solution)/shard_map/gather | solution.py:74
  692.2 9.5 all-gather.8
  702.8 7.8 fusion.8
  719.6 15.7 %all-gather.21.cloned.1.call-done = f32[8,1,36864]{2,1,0:T(1,128)} async-done(((f32[1,1,36864]{2,1,0:T(1,128)}), f32[8,1,36864]{2,1,0:T(1,128)}) %all-gather.21.cloned.1.call-update) | async-done | bytes 1179664 | tf_op jit(solution)/shard_map/all_gather | solution.py:54
  738.2 39.4 %psum.76 = f32[]{:T(128)} all-reduce(f32[]{:T(128)} %get-tuple-element.93), channel_id=1, replica_groups=mesh['row'=4,'col'=8] {'row','col'}, use_global_device_ids=true, to_apply=%region_23.24 | all-reduce | flops 1 | bytes 8 | tf_op jit(solution)/shard_map/psum | solution.py:79
  780.8 40.4 %psum.77 = f32[]{:T(128)} all-reduce(f32[]{:T(128)} %multiply_reduce_fusion.2), channel_id=1, replica_groups=mesh['row'=4,'col'=8] {'row','col'}, use_global_device_ids=true, to_apply=%region_25.26 | all-reduce | flops 1 | bytes 8 | tf_op jit(solution)/shard_map/psum | solution.py:79
  823.9 40.5 %psum.78 = f32[]{:T(128)} all-reduce(f32[]{:T(128)} %get-tuple-element.91), channel_id=1, replica_groups=mesh['row'=4,'col'=8] {'row','col'}, use_global_device_ids=true, to_apply=%region_27.28 | all-reduce | flops 1 | bytes 8 | tf_op jit(solution)/shard_map/psum | solution.py:79
  865.8 40.4 %psum.79 = f32[]{:T(128)} all-reduce(f32[]{:T(128)} %multiply_reduce_fusion), channel_id=1, replica_groups=mesh['row'=4,'col'=8] {'row','col'}, use_global_device_ids=true, to_apply=%region_29.30 | all-reduce | flops 1 | bytes 8 | tf_op jit(solution)/shard_map/psum | solution.py:64
  915.8 9.5 all-gather.10
  926.4 7.8 fusion.6
  936.5 21.6 %all-gather.23.cloned.1.call-done = f32[8,1,36864]{2,1,0:T(1,128)} async-done(((f32[1,1,36864]{2,1,0:T(1,128)}), f32[8,1,36864]{2,1,0:T(1,128)}) %all-gather.23.cloned.1.call-update) | async-done | bytes 1179664 | tf_op jit(solution)/shard_map/all_gather | solution.py:54
  (122 shorter events, 64.9 us)
Async XLA Ops:
  7.2 213.2 %all-gather.17.cloned.1.call-start = ((), (), s32[]{:S(2)}) async-start(), calls=%async_computation | async-start | bytes 1327104 | tf_op jit(solution)/shard_map/all_gather | solution.py:54
  69.3 75.9 %copy-start.1 = (s32[1,1,24]{2,1,0:T(1,128)S(1)}, s32[1,1,24]{2,1,0:T(1,128)}, u32[]{:S(2)}) copy-start(s32[1,1,24]{2,1,0:T(1,128)} %param.29) | copy-start | bytes 292
  153.3 33.7 %copy-start.2 = (s32[1,1,256]{2,1,0:T(1,128)S(1)}, s32[1,1,256]{2,1,0:T(1,128)}, u32[]{:S(2)}) copy-start(s32[1,1,256]{2,1,0:T(1,128)} %param.26) | copy-start | bytes 3076
  177.4 18.9 %copy-start.3 = (f32[1,1,256]{2,1,0:T(1,128)S(1)}, f32[1,1,256]{2,1,0:T(1,128)}, u32[]{:S(2)}) copy-start(f32[1,1,256]{2,1,0:T(1,128)} %param.24) | copy-start | bytes 3076
  177.4 21.3 %copy-start = (f32[1,1,4608]{2,1,0:T(1,128)S(1)}, f32[1,1,4608]{2,1,0:T(1,128)}, u32[]{:S(2)}) copy-start(f32[1,1,4608]{2,1,0:T(1,128)} %param.22) | copy-start | bytes 55300
  198.6 257.3 %all-gather.19.cloned.1.call-start = ((), (), s32[]{:S(2)}) async-start(), calls=%async_computation.1 | async-start | bytes 1327104 | tf_op jit(solution)/shard_map/all_gather | solution.py:54
  434.2 301.1 %all-gather.21.cloned.1.call-start = ((), (), s32[]{:S(2)}) async-start(), calls=%async_computation.2 | async-start | bytes 1327104 | tf_op jit(solution)/shard_map/all_gather | solution.py:54
  692.2 22.8 %copy-start.4 = (s32[2]{0:T(128)S(1)}, s32[2]{0:T(128)}, u32[]{:S(2)}) copy-start(s32[2]{0:T(128)} %constant.236.clone.1) | copy-start | bytes 28
  712.9 245.2 %all-gather.23.cloned.1.call-start = ((), (), s32[]{:S(2)}) async-start(), calls=%async_computation.3 | async-start | bytes 1327104 | tf_op jit(solution)/shard_map/all_gather | solution.py:54
Sparse Core Ops, SparseCore 0:
  198.7 21.5 all-gather.16
  434.3 21.4 all-gather.18
  713.1 22.1 all-gather.20
  936.6 21.4 all-gather.22
